TPU v7x, 128 devices: a whole 4x4x4 slice. The times are simulated.
128 devices in a mesh: row: 8 (over z, core), col: 16 (over x, y).
Axes of the slice: x: 4, y: 4, z: 4, core: 2. Of those that a mesh axis runs over, the one named last changes fastest.
Arguments:
- tokens: bfloat16 [1024, 12288], P('row', 'col'), may hold values from -6 to 6
- up_weight: bfloat16 [1024, 49152], P('row', 'col'), may hold values from -0.1875 to 0.1875
- down_weight: bfloat16 [1024, 49152], P('row', 'col'), may hold values from -0.09375 to 0.09375
- up_index: int32 [8, 384], P(None, 'col'), may hold values from 0 to 95, as said below
- down_index: int32 [8, 384], P(None, 'col'), may hold values from 0 to 95, as said below
- up_bias: float32 [49152], P('col'), may hold values from -3 to 3
- down_bias: float32 [12288], P('col'), may hold values from -3 to 3
Outputs:
- mixed: bfloat16 [1024, 12288], P('row', 'col')
Inputs may be any that keep to these rules, and one draw needn't show every extreme that they name: For each block column c the 8 entries up_index[:, c] are distinct, and for each slot s the entries over any 96 consecutive block columns are distinct. For each block row r the 8 entries down_index[:, r] are distinct, and for each slot s the entries over any 96 consecutive block rows are distinct.
All inputs are finite; a program needn't handle non-finite values.
Results may differ from a plain program's by a relative error of at most 0.015.
Values may be sent and summed in bfloat16 or wider, within the bound.
A program may use at most 128 MiB of HBM per device.

v0:
```python
import jax
import jax.numpy as jnp
from jax import lax
from jax.sharding import PartitionSpec as P

BLK = 128
KB = 8


def per_device(tokens, up_weight, down_weight, up_index, down_index, up_bias, down_bias):
    gathered = lax.all_gather(tokens, "col", axis=1, tiled=True)
    tok_rows = gathered.shape[0]
    dblocks = gathered.shape[1] // BLK
    features = gathered.reshape(tok_rows, dblocks, BLK)
    col_blocks = up_weight.shape[1] // BLK
    block_ids = jnp.arange(dblocks, dtype=jnp.int32)
    zero_pre = jnp.zeros((tok_rows, col_blocks, BLK), jnp.float32)
    running = zero_pre
    panel_rows = lax.all_gather(up_weight, "row", axis=0, tiled=True)
    block_count = panel_rows.shape[0] // BLK
    panels = panel_rows.reshape(block_count, BLK, col_blocks, BLK)
    for add_slot_index in range(block_count):
        selector = (up_index[add_slot_index][:, None] == block_ids[None, :]).astype(jnp.bfloat16)
        selected = jnp.einsum(
            "cd,tdk->tck", selector, features, preferred_element_type=jnp.float32
        ).astype(jnp.bfloat16)
        running = running + jnp.einsum(
            "tck,kcn->tcn", selected, panels[add_slot_index], preferred_element_type=jnp.float32
        )
    preact = running
    preact = preact + up_bias.reshape(col_blocks, BLK)[None]
    hidden = jax.nn.gelu(preact, approximate=True).astype(jnp.bfloat16)
    down_full = lax.all_gather(down_weight, "row", axis=0, tiled=True)
    down_grid = down_full.reshape(KB, BLK, col_blocks, BLK)
    totals = jnp.zeros((dblocks, tok_rows, BLK), jnp.float32)
    for slot_index in range(KB):
        product = jnp.einsum(
            "trk,nrk->rtn", hidden, down_grid[slot_index], preferred_element_type=jnp.float32
        )
        placer = (block_ids[:, None] == down_index[slot_index][None, :]).astype(jnp.float32)
        totals = totals + jnp.einsum(
            "dr,rtn->dtn",
            placer,
            product,
            precision=lax.Precision.HIGHEST,
            preferred_element_type=jnp.float32,
        )
    reduced = lax.psum_scatter(
        totals.astype(jnp.bfloat16), "col", scatter_dimension=0, tiled=True
    ).astype(jnp.float32)
    result = jnp.transpose(reduced, (1, 0, 2)).reshape(tok_rows, -1) + down_bias[None]
    return result.astype(jnp.bfloat16)


def solution(mesh):
    placed = (
        P("row", "col"),
        P("row", "col"),
        P("row", "col"),
        P(None, "col"),
        P(None, "col"),
        P("col"),
        P("col"),
    )
    return jax.shard_map(
        per_device, mesh=mesh, in_specs=placed, out_specs=P("row", "col"), check_vma=False
    )
```

profile of v0, /device:TPU:0, one launch (start us, length us, event | category | flops | bytes accessed | tf_op | source)
XLA Modules:
  0.0 308.1 jit_solution(4415510976900336198)
XLA Ops:
  6.5 0.7 all-gather.4.cloned.1.call-update
  7.3 2.3 copy.47
  9.7 1.2 copy.64
  11.0 49.1 %all-gather.4.cloned.1.call-done = bf16[128,12288]{1,0:T(8,128)(2,1)} async-done(((bf16[128,768]{1,0:T(8,128)(2,1)}), bf16[128,12288]{1,0:T(8,128)(2,1)}) %all-gather.4.cloned.1.call-update) | async-done | bytes 3145744 | tf_op jit(solution)/shard_map/all_gather | solution.py:11
  60.1 2.6 copy.100
  62.7 1.5 fusion.30
  64.2 1.5 fusion.28
  65.7 1.5 fusion.27
  69.6 1.5 fusion.29
  71.1 34.9 %all-gather.6.cloned.1.call-done = bf16[1024,3072]{0,1:T(8,128)(2,1)} async-done(((bf16[128,3072]{0,1:T(8,128)(2,1)}), bf16[1024,3072]{0,1:T(8,128)(2,1)}) %all-gather.6.cloned.1.call-update) | async-done | bytes 6291472 | tf_op jit(solution)/shard_map/all_gather | solution.py:19
  106.0 3.4 %fusion.96 = (bf16[128,3072]{0,1:T(8,128)(2,1)S(1)}, bf16[128,3072]{0,1:T(8,128)(2,1)S(1)}, bf16[128,3072]{0,1:T(8,128)(2,1)S(1)}, bf16[128,3072]{0,1:T(8,128)(2...) fusion(bf16[1024,3072]{0,1:T(8,128)(2,1)} %all-gather.6.cloned., ...), kind=kLoop, calls=%fused_computation.123 | loop fusion | bytes 12582912 | tf_op jit(solution)/shard_map/slice | solution.py:28
  110.6 0.7 fusion.34
  112.3 0.7 fusion.38
  113.0 0.7 fusion.40
  113.7 0.7 fusion.42
  114.3 0.7 fusion.44
  115.5 1.3 fusion.7
  116.7 37.0 %all-gather.8.cloned.1.call-done = bf16[1024,3072]{0,1:T(8,128)(2,1)} async-done(((bf16[128,3072]{0,1:T(8,128)(2,1)}), bf16[1024,3072]{0,1:T(8,128)(2,1)}) %all-gather.8.cloned.1.call-update) | async-done | bytes 6291472 | tf_op jit(solution)/shard_map/all_gather | solution.py:33
  153.7 3.4 %fusion.95 = (bf16[128,3072]{0,1:T(8,128)(2,1)S(1)}, bf16[128,3072]{0,1:T(8,128)(2,1)S(1)}, bf16[128,3072]{0,1:T(8,128)(2,1)S(1)}, bf16[128,3072]{0,1:T(8,128)(2...) fusion(bf16[1024,3072]{0,1:T(8,128)(2,1)} %all-gather.8.cloned., ...), kind=kLoop, calls=%fused_computation.122 | loop fusion | bytes 12582912 | tf_op jit(solution)/shard_map/slice | solution.py:38
  157.5 1.5 fusion.104
  161.3 5.7 %fusion.21 = f32[96,128,128]{2,0,1:T(8,128)} fusion(f32[24,128,128]{2,1,0:T(8,128)S(1)} %fusion.97, s32[24]{0:T(128)S(1)} %get-tuple-element.27), kind=kOutput, calls=%fused_computation.23 | convolution fusion | flops 452987136 | bytes 7864416 | tf_op jit(solution)/shard_map/dr,rtn->dtn/dot_general | solution.py:41
  167.0 5.5 %fusion.19 = f32[96,128,128]{2,0,1:T(8,128)} fusion(f32[24,128,128]{2,1,0:T(8,128)S(1)} %fusion.98, s32[24]{0:T(128)S(1)} %get-tuple-element.26), kind=kOutput, calls=%fused_computation.21 | convolution fusion | flops 452987136 | bytes 7864416 | tf_op jit(solution)/shard_map/dr,rtn->dtn/dot_general | solution.py:41
  172.5 5.5 %fusion.17 = f32[96,128,128]{2,0,1:T(8,128)} fusion(f32[24,128,128]{2,1,0:T(8,128)S(1)} %fusion.99, s32[24]{0:T(128)S(1)} %get-tuple-element.25), kind=kOutput, calls=%fused_computation.19 | convolution fusion | flops 452987136 | bytes 7864416 | tf_op jit(solution)/shard_map/dr,rtn->dtn/dot_general | solution.py:41
  178.0 5.5 %fusion.15 = f32[96,128,128]{2,0,1:T(8,128)} fusion(f32[24,128,128]{2,1,0:T(8,128)S(1)} %fusion.100, s32[24]{0:T(128)S(1)} %get-tuple-element.24), kind=kOutput, calls=%fused_computation.17 | convolution fusion | flops 452987136 | bytes 7864416 | tf_op jit(solution)/shard_map/dr,rtn->dtn/dot_general | solution.py:41
  183.5 5.4 %fusion.13 = f32[96,128,128]{2,0,1:T(8,128)} fusion(f32[24,128,128]{2,1,0:T(8,128)S(1)} %fusion.101, s32[24]{0:T(128)S(1)} %get-tuple-element.23), kind=kOutput, calls=%fused_computation.15 | convolution fusion | flops 452987136 | bytes 7864416 | tf_op jit(solution)/shard_map/dr,rtn->dtn/dot_general | solution.py:41
  189.0 5.5 %fusion.11 = f32[96,128,128]{2,0,1:T(8,128)} fusion(f32[24,128,128]{2,1,0:T(8,128)S(1)} %fusion.102, s32[24]{0:T(128)S(1)} %get-tuple-element.22), kind=kOutput, calls=%fused_computation.13 | convolution fusion | flops 452987136 | bytes 7864416 | tf_op jit(solution)/shard_map/dr,rtn->dtn/dot_general | solution.py:41
  194.4 5.5 %fusion.9 = f32[96,128,128]{2,0,1:T(8,128)} fusion(f32[24,128,128]{2,1,0:T(8,128)S(1)} %fusion.103, s32[24]{0:T(128)S(1)} %get-tuple-element.28), kind=kOutput, calls=%fused_computation.11 | convolution fusion | flops 452987136 | bytes 7864416 | tf_op jit(solution)/shard_map/dr,rtn->dtn/dot_general | solution.py:41
  199.9 20.0 %add_convert_fusion = bf16[96,128,128]{2,0,1:T(8,128)(2,1)S(1)} fusion(f32[96,128,128]{2,0,1:T(8,128)} %fusion.9, f32[96,128,128]{2,0,1:T(8,128)} %fusion.11, f32[96,128,128]{2,0,1:T(8,128)} %fusion.13, f32[96,128,128]{2,0,1:T(8,128)} %fusion.15, f32[96,128,128]{2,0,1:T(8,128)} %fusion.17, f32[96,128,128]{2,0,1:T(8,128)} %fusion.21, ...), kind=kOutput, calls=%fused_computation | convolution fusion | flops 465570048 | bytes 48758880 | tf_op jit(solution)/shard_map/dr,rtn->dtn/dot_general | solution.py:41
  219.9 2.9 copy.81
  222.8 76.7 %reduce-scatter.2.cloned.1.call-done = bf16[6,128,128]{2,1,0:T(8,128)(2,1)} async-done(((bf16[96,128,128]{2,1,0:T(8,128)(2,1)}), bf16[6,128,128]{2,1,0:T(8,128)(2,1)}) %reduce-scatter.2.cloned.1.call-update) | async-done | bytes 196624 | tf_op jit(solution)/shard_map/reduce_scatter | solution.py:48
  299.5 1.1 copy.82
  300.8 0.8 copy.83
  (41 shorter events, 8.1 us)
Async XLA Ops:
  6.5 3.2 %copy-start.4 = (bf16[128,3072]{1,0:T(8,128)(2,1)S(1)}, bf16[128,3072]{1,0:T(8,128)(2,1)}, u32[]{:S(2)}) copy-start(bf16[128,3072]{1,0:T(8,128)(2,1)} %param.9) | copy-start | bytes 2359300
  6.5 53.6 %all-gather.4.cloned.1.call-start = ((), (), s32[]{:S(2)}) async-start(), calls=%async_computation.1 | async-start | bytes 3342336 | tf_op jit(solution)/shard_map/all_gather | solution.py:11
  7.3 98.7 %all-gather.6.cloned.1.call-start = ((), (), s32[]{:S(2)}) async-start(), calls=%async_computation.2 | async-start | bytes 7077888 | tf_op jit(solution)/shard_map/all_gather | solution.py:19
  9.6 1.3 copy-start.7
  9.6 1.4 copy-start.8
  9.6 144.1 %all-gather.8.cloned.1.call-start = ((), (), s32[]{:S(2)}) async-start(), calls=%async_computation.3 | async-start | bytes 7077888 | tf_op jit(solution)/shard_map/all_gather | solution.py:33
  10.9 288.6 %reduce-scatter.2.cloned.1.call-start = ((), (), s32[]{:S(2)}) async-start(), calls=%async_computation.4 | async-start | bytes 3342336 | tf_op jit(solution)/shard_map/reduce_scatter | solution.py:48
  106.0 3.4 %copy-start.2 = (bf16[128,24,128]{2,1,0:T(8,128)(2,1)S(1)}, bf16[128,24,128]{2,1,0:T(8,128)(2,1)}, u32[]{:S(2)}) copy-start(bf16[128,24,128]{2,1,0:T(8,128)(2,1)} %fusion.29) | copy-start | bytes 2359300
  109.4 1.1 copy-start.1
  110.6 1.1 copy-start
  114.3 1.1 copy-start.3
  114.3 1.1 copy-start.5
  222.8 77.8 %copy-start.6 = (f32[768]{0:T(1024)S(1)}, f32[768]{0:T(1024)}, u32[]{:S(2)}) copy-start(f32[768]{0:T(1024)} %param.13) | copy-start | bytes 9220
Sparse Core Ops, SparseCore 0:
  9.6 50.4 all-gather.3
  61.8 44.1 all-gather.5
  107.7 46.0 all-gather.7
  222.9 76.5 reduce-scatter.1
where the time goes:
time: 308 us
  waiting for transfers between devices  198 us (64%)
  matrix products  77 us (25%)
  local copies, waits for them, and re-layouts  19.1 us (6%)
  between operations  13.3 us (4%)
    reduce_scatter x1, waiting for transfers between devices, per_device(): lax.psum_scatter(totals.astype(jnp.bfloat16), 'col', scatter_dimension=0,...  76.7 us
    dot_general x8, matrix products, per_device(): jnp.einsum('dr,rtn->dtn', placer, product, precision=lax.Precision.HIGHES...  58.6 us
    all_gather x1, waiting for transfers between devices, per_device(): gathered = lax.all_gather(tokens, 'col', axis=1, tiled=True)  49.1 us
    all_gather x1, waiting for transfers between devices, per_device(): down_full = lax.all_gather(down_weight, 'row', axis=0, tiled=True)  37 us
    all_gather x1, waiting for transfers between devices, per_device(): panel_rows = lax.all_gather(up_weight, 'row', axis=0, tiled=True)  34.9 us
    dot_general x8, matrix products, per_device(): jnp.einsum('cd,tdk->tck', selector, features, preferred_element_type=jnp....  8.36 us
    unnamed x21, local copies, waits for them, and re-layouts  7.5 us
  transfers between devices with their start and end apart: 4, of which 4 were waited for; matrix products, arithmetic and copies ran while one was open for 8% of the time, Pallas kernels for 0%

commit v1 on v0

--- a/solution.py
+++ b/solution.py
@@ -8,7 +8,11 @@
 
 
 def per_device(tokens, up_weight, down_weight, up_index, down_index, up_bias, down_bias):
-    gathered = lax.all_gather(tokens, "col", axis=1, tiled=True)
+    peers = lax.axis_size("col")
+    repeats = [peers if d == 1 else 1 for d in range(tokens.ndim)]
+    gathered = lax.all_to_all(
+        jnp.tile(tokens, repeats), "col", split_axis=1, concat_axis=1, tiled=True
+    )
     tok_rows = gathered.shape[0]
     dblocks = gathered.shape[1] // BLK
     features = gathered.reshape(tok_rows, dblocks, BLK)

time: 308 us -> 259 us (0.84)
  waiting for transfers between devices: 198 us -> 128 us
  local copies, waits for them, and re-layouts: 19.1 us -> 29.3 us
  starting transfers between devices: 0.13 us -> 7.33 us
  matrix products: 77 us -> 80.6 us
    all_gather x1 -> x0, waiting for transfers between devices: 49.1 us -> none  [per_device(): gathered = lax.all_gather(tokens, 'col', axis=1, tiled=True)]
    all_to_all x0 -> x1, waiting for transfers between devices: none -> 42.4 us  [per_device(): lax.all_to_all(jnp.tile(tokens, repeats), 'col', split_axis=1, concat_axi...]
    all_gather x1, waiting for transfers between devices: 34.9 us -> 0.01 us  [per_device(): panel_rows = lax.all_gather(up_weight, 'row', axis=0, tiled=True)]
    all_gather x1, waiting for transfers between devices: 37 us -> 9.05 us  [per_device(): down_full = lax.all_gather(down_weight, 'row', axis=0, tiled=True)]
    all_to_all x0 -> x1, starting transfers between devices: none -> 7.25 us  [per_device(): lax.all_to_all(jnp.tile(tokens, repeats), 'col', split_axis=1, concat_axi...]
    reshape x0 -> x1, local copies, waits for them, and re-layouts: none -> 5.17 us  [per_device(): features = gathered.reshape(tok_rows, dblocks, BLK)]
    dot_general x8, matrix products: 8.36 us -> 11.9 us  [per_device(): jnp.einsum('cd,tdk->tck', selector, features, preferred_element_type=jnp....]
    all_to_all x0 -> x1, local copies, waits for them, and re-layouts: none -> 3.39 us  [per_device(): lax.all_to_all(jnp.tile(tokens, repeats), 'col', split_axis=1, concat_axi...]
  transfers between devices with their start and end apart: 4 -> 4, of which waited for: 4 -> 3; matrix products, arithmetic and copies ran while one was open for 8% -> 13% of each run, Pallas kernels for 0% -> 0%
where the time goes in v1:
time: 259 us
  waiting for transfers between devices  128 us (49%)
  matrix products  80.6 us (31%)
  local copies, waits for them, and re-layouts  29.3 us (11%)
  between operations  13.3 us (5%)
  starting transfers between devices  7.33 us (3%)
    reduce_scatter x1, waiting for transfers between devices, per_device(): lax.psum_scatter(totals.astype(jnp.bfloat16), 'col', scatter_dimension=0,...  76.7 us
    dot_general x8, matrix products, per_device(): jnp.einsum('dr,rtn->dtn', placer, product, precision=lax.Precision.HIGHES...  58.6 us
    all_to_all x1, waiting for transfers between devices, per_device(): lax.all_to_all(jnp.tile(tokens, repeats), 'col', split_axis=1, concat_axi...  42.4 us
    dot_general x8, matrix products, per_device(): jnp.einsum('cd,tdk->tck', selector, features, preferred_element_type=jnp....  11.9 us
    all_gather x1, waiting for transfers between devices, per_device(): down_full = lax.all_gather(down_weight, 'row', axis=0, tiled=True)  9.05 us
    all_to_all x1, starting transfers between devices, per_device(): lax.all_to_all(jnp.tile(tokens, repeats), 'col', split_axis=1, concat_axi...  7.25 us
    unnamed x30, local copies, waits for them, and re-layouts  6.92 us
    dot_general x8, matrix products, per_device(): jnp.einsum('tck,kcn->tcn', selected, panels[add_slot_index], preferred_el...  5.84 us
  transfers between devices with their start and end apart: 4, of which 3 were waited for; matrix products, arithmetic and copies ran while one was open for 13% of the time, Pallas kernels for 0%

profile of v1, /device:TPU:0, one launch (start us, length us, event | category | flops | bytes accessed | tf_op | source)
XLA Modules:
  0.0 258.8 jit_solution(4070106358747659434)
XLA Ops:
  6.5 2.4 copy.49
  9.0 1.2 copy.66
  10.2 2.0 tile.2
  12.1 7.2 %all-to-all-start = ((bf16[128,16,768]{2,0,1:T(8,128)(2,1)}), bf16[128,16,768]{2,0,1:T(8,128)(2,1)S(1)}, u32[]{:S(2)}, u32[]{:S(2)}) async-start(bf16[128,16,768]{2,0,1:T(8,128)(2,1)} %tile.2), calls=%async_computation | async-start | bytes 6291456 | tf_op jit(solution)/shard_map/all_to_all | solution.py:13
  19.5 42.4 %all-to-all-done = bf16[128,16,768]{2,0,1:T(8,128)(2,1)S(1)} async-done(((bf16[128,16,768]{2,0,1:T(8,128)(2,1)}), bf16[128,16,768]{2,0,1:T(8,128)(2,1)S(1)}, u32[]{:S(2)}, u32[]{:S(2)}) %all-to-all-start) | async-done | bytes 3145760 | tf_op jit(solution)/shard_map/all_to_all | solution.py:13
  61.9 3.4 %copy.48 = bf16[128,16,768]{2,1,0:T(8,128)(2,1)} copy(bf16[128,16,768]{2,0,1:T(8,128)(2,1)S(1)} %all-to-all-done) | data formatting | bytes 6291456 | tf_op jit(solution)/shard_map/all_to_all | solution.py:13
  65.3 5.2 %reshape.61 = bf16[128,96,128]{2,1,0:T(8,128)(2,1)S(1)} reshape(bf16[128,16,768]{2,1,0:T(8,128)(2,1)} %copy.48) | data formatting | bytes 6291456 | tf_op jit(solution)/shard_map/reshape | solution.py:18
  70.4 1.5 fusion.30
  72.0 1.5 fusion.29
  73.5 1.5 fusion.28
  75.0 1.5 fusion.27
  76.5 1.5 fusion.26
  77.9 1.5 fusion.25
  79.4 1.5 fusion.24
  80.9 1.5 fusion.23
  82.4 3.7 %fusion.96 = (bf16[128,3072]{0,1:T(8,128)(2,1)S(1)}, bf16[128,3072]{0,1:T(8,128)(2,1)S(1)}, bf16[128,3072]{0,1:T(8,128)(2,1)S(1)}, bf16[128,3072]{0,1:T(8,128)(2...) fusion(bf16[1024,3072]{0,1:T(8,128)(2,1)} %all-gather.3.cloned., ...), kind=kLoop, calls=%fused_computation.123 | loop fusion | bytes 12582912 | tf_op jit(solution)/shard_map/slice | solution.py:32
  94.1 1.3 fusion.7
  95.4 9.1 %all-gather.5.cloned.1.call-done = bf16[1024,3072]{0,1:T(8,128)(2,1)} async-done(((bf16[128,3072]{0,1:T(8,128)(2,1)}), bf16[1024,3072]{0,1:T(8,128)(2,1)}) %all-gather.5.cloned.1.call-update) | async-done | bytes 6291472 | tf_op jit(solution)/shard_map/all_gather | solution.py:37
  104.4 3.4 %fusion.95 = (bf16[128,3072]{0,1:T(8,128)(2,1)S(1)}, bf16[128,3072]{0,1:T(8,128)(2,1)S(1)}, bf16[128,3072]{0,1:T(8,128)(2,1)S(1)}, bf16[128,3072]{0,1:T(8,128)(2...) fusion(bf16[1024,3072]{0,1:T(8,128)(2,1)} %all-gather.5.cloned., ...), kind=kLoop, calls=%fused_computation.122 | loop fusion | bytes 12582912 | tf_op jit(solution)/shard_map/slice | solution.py:42
  107.8 1.5 fusion.104
  112.0 5.7 %fusion.21 = f32[96,128,128]{2,0,1:T(8,128)} fusion(f32[24,128,128]{2,1,0:T(8,128)S(1)} %fusion.97, s32[24]{0:T(128)S(1)} %get-tuple-element.27), kind=kOutput, calls=%fused_computation.23 | convolution fusion | flops 452987136 | bytes 7864416 | tf_op jit(solution)/shard_map/dr,rtn->dtn/dot_general | solution.py:45
  117.8 5.5 %fusion.19 = f32[96,128,128]{2,0,1:T(8,128)} fusion(f32[24,128,128]{2,1,0:T(8,128)S(1)} %fusion.98, s32[24]{0:T(128)S(1)} %get-tuple-element.26), kind=kOutput, calls=%fused_computation.21 | convolution fusion | flops 452987136 | bytes 7864416 | tf_op jit(solution)/shard_map/dr,rtn->dtn/dot_general | solution.py:45
  123.2 5.5 %fusion.17 = f32[96,128,128]{2,0,1:T(8,128)} fusion(f32[24,128,128]{2,1,0:T(8,128)S(1)} %fusion.99, s32[24]{0:T(128)S(1)} %get-tuple-element.25), kind=kOutput, calls=%fused_computation.19 | convolution fusion | flops 452987136 | bytes 7864416 | tf_op jit(solution)/shard_map/dr,rtn->dtn/dot_general | solution.py:45
  128.7 5.5 %fusion.15 = f32[96,128,128]{2,0,1:T(8,128)} fusion(f32[24,128,128]{2,1,0:T(8,128)S(1)} %fusion.100, s32[24]{0:T(128)S(1)} %get-tuple-element.24), kind=kOutput, calls=%fused_computation.17 | convolution fusion | flops 452987136 | bytes 7864416 | tf_op jit(solution)/shard_map/dr,rtn->dtn/dot_general | solution.py:45
  134.2 5.4 %fusion.13 = f32[96,128,128]{2,0,1:T(8,128)} fusion(f32[24,128,128]{2,1,0:T(8,128)S(1)} %fusion.101, s32[24]{0:T(128)S(1)} %get-tuple-element.23), kind=kOutput, calls=%fused_computation.15 | convolution fusion | flops 452987136 | bytes 7864416 | tf_op jit(solution)/shard_map/dr,rtn->dtn/dot_general | solution.py:45
  139.7 5.5 %fusion.11 = f32[96,128,128]{2,0,1:T(8,128)} fusion(f32[24,128,128]{2,1,0:T(8,128)S(1)} %fusion.102, s32[24]{0:T(128)S(1)} %get-tuple-element.22), kind=kOutput, calls=%fused_computation.13 | convolution fusion | flops 452987136 | bytes 7864416 | tf_op jit(solution)/shard_map/dr,rtn->dtn/dot_general | solution.py:45
  145.1 5.5 %fusion.9 = f32[96,128,128]{2,0,1:T(8,128)} fusion(f32[24,128,128]{2,1,0:T(8,128)S(1)} %fusion.103, s32[24]{0:T(128)S(1)} %get-tuple-element.28), kind=kOutput, calls=%fused_computation.11 | convolution fusion | flops 452987136 | bytes 7864416 | tf_op jit(solution)/shard_map/dr,rtn->dtn/dot_general | solution.py:45
  150.6 20.0 %add_convert_fusion = bf16[96,128,128]{2,0,1:T(8,128)(2,1)S(1)} fusion(f32[96,128,128]{2,0,1:T(8,128)} %fusion.9, f32[96,128,128]{2,0,1:T(8,128)} %fusion.11, f32[96,128,128]{2,0,1:T(8,128)} %fusion.13, f32[96,128,128]{2,0,1:T(8,128)} %fusion.15, f32[96,128,128]{2,0,1:T(8,128)} %fusion.17, f32[96,128,128]{2,0,1:T(8,128)} %fusion.21, ...), kind=kOutput, calls=%fused_computation | convolution fusion | flops 465570048 | bytes 48758880 | tf_op jit(solution)/shard_map/dr,rtn->dtn/dot_general | solution.py:45
  170.6 2.8 %copy.83 = bf16[96,128,128]{2,1,0:T(8,128)(2,1)} copy(bf16[96,128,128]{2,0,1:T(8,128)(2,1)S(1)} %add_convert_fusion) | data formatting | bytes 6291456 | tf_op jit(solution)/shard_map/convert_element_type | solution.py:53
  173.5 76.7 %reduce-scatter.2.cloned.1.call-done = bf16[6,128,128]{2,1,0:T(8,128)(2,1)} async-done(((bf16[96,128,128]{2,1,0:T(8,128)(2,1)}), bf16[6,128,128]{2,1,0:T(8,128)(2,1)}) %reduce-scatter.2.cloned.1.call-update) | async-done | bytes 196624 | tf_op jit(solution)/shard_map/reduce_scatter | solution.py:52
  250.2 1.1 copy.84
  251.4 0.8 copy.85
  (52 shorter events, 11.0 us)
Async XLA Ops:
  6.5 2.4 copy-start.8
  6.5 75.8 %all-gather.3.cloned.1.call-start = ((), (), s32[]{:S(2)}) async-start(), calls=%async_computation.2 | async-start | bytes 7077888 | tf_op jit(solution)/shard_map/all_gather | solution.py:23
  8.9 1.3 copy-start.9
  8.9 95.5 %all-gather.5.cloned.1.call-start = ((), (), s32[]{:S(2)}) async-start(), calls=%async_computation.3 | async-start | bytes 7077888 | tf_op jit(solution)/shard_map/all_gather | solution.py:37
  12.1 7.3 %copy-start.12 = (s32[8,24]{1,0:T(8,128)S(1)}, s32[8,24]{1,0:T(8,128)}, u32[]{:S(2)}) copy-start(s32[8,24]{1,0:T(8,128)} %param.10) | copy-start | bytes 2308
  12.1 7.3 %copy-start.13 = (s32[8,24]{1,0:T(8,128)S(1)}, s32[8,24]{1,0:T(8,128)}, u32[]{:S(2)}) copy-start(s32[8,24]{1,0:T(8,128)} %param.11) | copy-start | bytes 2308
  12.1 49.7 %all-to-all-start = ((bf16[128,16,768]{2,0,1:T(8,128)(2,1)}), bf16[128,16,768]{2,0,1:T(8,128)(2,1)S(1)}, u32[]{:S(2)}, u32[]{:S(2)}) async-start(bf16[128,16,768]{2,0,1:T(8,128)(2,1)} %tile.2), calls=%async_computation | async-start | bytes 6291456 | tf_op jit(solution)/shard_map/all_to_all | solution.py:13
  19.4 230.8 %reduce-scatter.2.cloned.1.call-start = ((), (), s32[]{:S(2)}) async-start(), calls=%async_computation.4 | async-start | bytes 3342336 | tf_op jit(solution)/shard_map/reduce_scatter | solution.py:52
  82.4 3.7 %copy-start.6 = (bf16[128,24,128]{2,1,0:T(8,128)(2,1)S(1)}, bf16[128,24,128]{2,1,0:T(8,128)(2,1)}, u32[]{:S(2)}) copy-start(bf16[128,24,128]{2,1,0:T(8,128)(2,1)} %fusion.29) | copy-start | bytes 2359300
  86.1 1.1 copy-start.5
  87.3 1.1 copy-start.3
  88.4 1.1 copy-start.2
  89.5 1.1 copy-start.1
  90.7 1.1 copy-start.4
  91.8 1.1 copy-start
  92.9 1.2 copy-start.7
  92.9 1.2 copy-start.10
  173.5 77.8 %copy-start.11 = (f32[768]{0:T(1024)S(1)}, f32[768]{0:T(1024)}, u32[]{:S(2)}) copy-start(f32[768]{0:T(1024)} %param.13) | copy-start | bytes 9220
Sparse Core Ops, SparseCore 0:
  9.0 47.6 all-gather.2
  58.4 45.9 all-gather.4
  173.6 76.4 reduce-scatter.1
